TPU v7x, 32 devices: a whole 2x2x4 slice. The times are simulated.
32 devices in a mesh: dp: 4 (over x, core), fsdp: 8 (over z, y).
Axes of the slice: x: 2, y: 2, z: 4, core: 2. Of those that a mesh axis runs over, the one named last changes fastest.
Arguments:
- tokens: bfloat16 [32768, 768], P(('dp', 'fsdp')), may hold values from -6 to 6
- segment_ids: int32 [64, 512], P(('dp', 'fsdp')), may hold values from 0 to 7, never falling along the last dimension, each value on 1 to 160 neighbouring positions
- query_weight: bfloat16 [768, 768], P('fsdp'), may hold values from -0.21875 to 0.21875
- query_bias: bfloat16 [768], P('fsdp'), may hold values from -3 to 3
- key_weight: bfloat16 [768, 768], P('fsdp'), may hold values from -0.21875 to 0.21875
- value_weight: bfloat16 [768, 768], P('fsdp'), may hold values from -0.21875 to 0.21875
- value_bias: bfloat16 [768], P('fsdp'), may hold values from -3 to 3
- out_weight: bfloat16 [768, 768], P('fsdp'), may hold values from -0.625 to 0.625
- out_bias: bfloat16 [768], P('fsdp'), may hold values from -3 to 3
- first_gain: bfloat16 [768], P('fsdp'), may hold values from 0.25 to 1.75
- first_shift: bfloat16 [768], P('fsdp'), may hold values from -3 to 3
- expand_weight: bfloat16 [768, 3072], P('fsdp'), may hold values from -0.21875 to 0.21875
- expand_bias: bfloat16 [3072], P('fsdp'), may hold values from -3 to 3
- reduce_weight: bfloat16 [3072, 768], P('fsdp'), may hold values from -0.109375 to 0.109375
- reduce_bias: bfloat16 [768], P('fsdp'), may hold values from -3 to 3
- second_gain: bfloat16 [768], P('fsdp'), may hold values from 0.25 to 1.75
- second_shift: bfloat16 [768], P('fsdp'), may hold values from -3 to 3
- cotangent: bfloat16 [32768, 768], P(('dp', 'fsdp')), may hold values from -6 to 6
Outputs:
- output: bfloat16 [32768, 768], P(('dp', 'fsdp'))
- input_grad: float32 [32768, 768], P(('dp', 'fsdp'))
- grad_query_weight: float32 [768, 768], P('fsdp')
- grad_query_bias: float32 [768], P('fsdp')
- grad_key_weight: float32 [768, 768], P('fsdp')
- grad_value_weight: float32 [768, 768], P('fsdp')
- grad_value_bias: float32 [768], P('fsdp')
- grad_out_weight: float32 [768, 768], P('fsdp')
- grad_out_bias: float32 [768], P('fsdp')
- grad_first_gain: float32 [768], P('fsdp')
- grad_first_shift: float32 [768], P('fsdp')
- grad_expand_weight: float32 [768, 3072], P('fsdp')
- grad_expand_bias: float32 [3072], P('fsdp')
- grad_reduce_weight: float32 [3072, 768], P('fsdp')
- grad_reduce_bias: float32 [768], P('fsdp')
- grad_second_gain: float32 [768], P('fsdp')
- grad_second_shift: float32 [768], P('fsdp')
Inputs may be any that keep to these rules, and one draw needn't show every extreme that they name: `segment_ids`: within a sequence the fragment numbers never fall; every one of the 8 fragments is present, and the longest has exactly 160 tokens.
All inputs are finite; a program needn't handle non-finite values.
Results may differ from a plain program's by a relative error of at most 0.02.
Values may be sent and summed in bfloat16 or wider, within the bound.
A program may use at most 192 MiB of HBM per device.

v0:
```python
import jax
import jax.numpy as jnp
from jax import lax
from jax.sharding import PartitionSpec as P

HEADS = 12
HEAD = 64


def layer_norm(rows, gain, shift):
    average = jnp.mean(rows, axis=-1, keepdims=True)
    centered = rows - average
    rescale = lax.rsqrt(jnp.mean(centered * centered, axis=-1, keepdims=True) + 1e-12)
    normed = centered * rescale
    return (normed * gain.astype(jnp.float32) + shift.astype(jnp.float32), normed, rescale)


def norm_back(gradient, normed, rescale, gain):
    scaled = gradient * gain.astype(jnp.float32)
    inner_mean = jnp.mean(scaled * normed, axis=-1, keepdims=True)
    rows_grad = rescale * (scaled - jnp.mean(scaled, axis=-1, keepdims=True) - normed * inner_mean)
    return (rows_grad, jnp.sum(gradient * normed, axis=0), jnp.sum(gradient, axis=0))


def linear(rows, weight, bias):
    return jnp.dot(rows, weight, preferred_element_type=jnp.float32) + bias.astype(jnp.float32)


def weight_grad(rows, gradient):
    return jnp.einsum("ti,to->io", rows, gradient, preferred_element_type=jnp.float32)


def bias_grad(gradient):
    return jnp.sum(gradient.astype(jnp.float32), axis=0)


def back_rows(gradient, weight):
    return jnp.einsum("to,io->ti", gradient, weight, preferred_element_type=jnp.float32)


def gelu_slope(inner):
    normal_cdf = 0.5 * (1.0 + lax.erf(inner * 0.7071067811865476))
    density = jnp.exp(-0.5 * inner * inner) * 0.3989422804014327
    return normal_cdf + inner * density


def masked_scores(queries, key_rows, fragment):
    scaling = queries.shape[-1] ** (-0.5)
    scores = (
        jnp.einsum("qhd,khd->hqk", queries, key_rows, preferred_element_type=jnp.float32) * scaling
    )
    same_fragment = fragment[:, None] == fragment[None, :]
    return jnp.where(same_fragment[None, :, :], scores, -1000000000.0)


def attend_forward(bundle):
    queries, key_rows, value_rows, fragment = bundle
    scores = masked_scores(queries, key_rows, fragment)
    highest = jnp.max(scores, axis=-1, keepdims=True)
    lifted = jnp.exp(scores - highest)
    totals = jnp.sum(lifted, axis=-1, keepdims=True)
    weights = (lifted / totals).astype(jnp.bfloat16)
    mixed = jnp.einsum("hqk,khd->qhd", weights, value_rows, preferred_element_type=jnp.float32)
    return (mixed.astype(jnp.bfloat16), highest + jnp.log(totals))


def attend_backward(bundle):
    queries, key_rows, value_rows, fragment, mixed_grad, log_totals = bundle
    scaling = queries.shape[-1] ** (-0.5)
    weights = jnp.exp(masked_scores(queries, key_rows, fragment) - log_totals)
    value_grad = jnp.einsum(
        "hqk,qhd->khd", weights.astype(jnp.bfloat16), mixed_grad, preferred_element_type=jnp.float32
    )
    prob_grad = jnp.einsum(
        "qhd,khd->hqk", mixed_grad, value_rows, preferred_element_type=jnp.float32
    )
    score_grad = (
        weights * (prob_grad - jnp.sum(prob_grad * weights, axis=-1, keepdims=True))
    ).astype(jnp.bfloat16)
    query_grad = (
        jnp.einsum("hqk,khd->qhd", score_grad, key_rows, preferred_element_type=jnp.float32)
        * scaling
    )
    key_grad = (
        jnp.einsum("hqk,qhd->khd", score_grad, queries, preferred_element_type=jnp.float32)
        * scaling
    )
    return (
        query_grad.astype(jnp.bfloat16),
        key_grad.astype(jnp.bfloat16),
        value_grad.astype(jnp.bfloat16),
    )


def on_device(
    tokens,
    segment_ids,
    query_weight,
    query_bias,
    key_weight,
    value_weight,
    value_bias,
    out_weight,
    out_bias,
    first_gain,
    first_shift,
    expand_weight,
    expand_bias,
    reduce_weight,
    reduce_bias,
    second_gain,
    second_shift,
    cotangent,
):
    seq_count, seq_length = segment_ids.shape
    shaped = (seq_count, seq_length, HEADS, HEAD)
    attention_set = (
        lax.all_gather(query_weight, "fsdp", axis=0, tiled=True),
        lax.all_gather(query_bias, "fsdp", axis=0, tiled=True),
        lax.all_gather(key_weight, "fsdp", axis=0, tiled=True),
        lax.all_gather(value_weight, "fsdp", axis=0, tiled=True),
        lax.all_gather(value_bias, "fsdp", axis=0, tiled=True),
        lax.all_gather(out_weight, "fsdp", axis=0, tiled=True),
        lax.all_gather(out_bias, "fsdp", axis=0, tiled=True),
        lax.all_gather(first_gain, "fsdp", axis=0, tiled=True),
        lax.all_gather(first_shift, "fsdp", axis=0, tiled=True),
    )
    queries = (
        linear(tokens, attention_set[0], attention_set[1]).astype(jnp.bfloat16).reshape(shaped)
    )
    key_rows = (
        jnp.dot(tokens, attention_set[2], preferred_element_type=jnp.float32)
        .astype(jnp.bfloat16)
        .reshape(shaped)
    )
    value_rows = (
        linear(tokens, attention_set[3], attention_set[4]).astype(jnp.bfloat16).reshape(shaped)
    )
    mixed, log_totals = lax.map(attend_forward, (queries, key_rows, value_rows, segment_ids))
    mixed = mixed.reshape(tokens.shape)
    first_sum = tokens.astype(jnp.float32) + linear(mixed, attention_set[5], attention_set[6])
    hidden, first_normed, first_rescale = layer_norm(first_sum, attention_set[7], attention_set[8])
    hidden_low = hidden.astype(jnp.bfloat16)
    feed_set = (
        lax.all_gather(expand_weight, "fsdp", axis=0, tiled=True),
        lax.all_gather(expand_bias, "fsdp", axis=0, tiled=True),
        lax.all_gather(reduce_weight, "fsdp", axis=0, tiled=True),
        lax.all_gather(reduce_bias, "fsdp", axis=0, tiled=True),
        lax.all_gather(second_gain, "fsdp", axis=0, tiled=True),
        lax.all_gather(second_shift, "fsdp", axis=0, tiled=True),
    )
    inner = linear(hidden_low, feed_set[0], feed_set[1])
    active = jax.nn.gelu(inner, approximate=False).astype(jnp.bfloat16)
    second_sum = hidden + linear(active, feed_set[2], feed_set[3])
    output, second_normed, second_rescale = layer_norm(second_sum, feed_set[4], feed_set[5])
    feed_back = (
        lax.all_gather(expand_weight, "fsdp", axis=0, tiled=True),
        lax.all_gather(expand_bias, "fsdp", axis=0, tiled=True),
        lax.all_gather(reduce_weight, "fsdp", axis=0, tiled=True),
        lax.all_gather(reduce_bias, "fsdp", axis=0, tiled=True),
        lax.all_gather(second_gain, "fsdp", axis=0, tiled=True),
        lax.all_gather(second_shift, "fsdp", axis=0, tiled=True),
    )
    second_grad, grad_second_gain, grad_second_shift = norm_back(
        cotangent.astype(jnp.float32), second_normed, second_rescale, feed_back[4]
    )
    branch_grad = second_grad.astype(jnp.bfloat16)
    grad_reduce = weight_grad(active, branch_grad)
    grad_reduce_bias = bias_grad(branch_grad)
    inner_grad = (back_rows(branch_grad, feed_back[2]) * gelu_slope(inner)).astype(jnp.bfloat16)
    grad_expand = weight_grad(hidden_low, inner_grad)
    grad_expand_bias = bias_grad(inner_grad)
    hidden_grad = second_grad + back_rows(inner_grad, feed_back[0])
    feed_grads = (
        lax.psum_scatter(
            grad_expand.astype(jnp.bfloat16), "fsdp", scatter_dimension=0, tiled=True
        ).astype(jnp.float32),
        lax.psum_scatter(
            grad_expand_bias.astype(jnp.bfloat16), "fsdp", scatter_dimension=0, tiled=True
        ).astype(jnp.float32),
        lax.psum_scatter(
            grad_reduce.astype(jnp.bfloat16), "fsdp", scatter_dimension=0, tiled=True
        ).astype(jnp.float32),
        lax.psum_scatter(
            grad_reduce_bias.astype(jnp.bfloat16), "fsdp", scatter_dimension=0, tiled=True
        ).astype(jnp.float32),
        lax.psum_scatter(
            grad_second_gain.astype(jnp.bfloat16), "fsdp", scatter_dimension=0, tiled=True
        ).astype(jnp.float32),
        lax.psum_scatter(
            grad_second_shift.astype(jnp.bfloat16), "fsdp", scatter_dimension=0, tiled=True
        ).astype(jnp.float32),
    )
    attention_back = (
        lax.all_gather(query_weight, "fsdp", axis=0, tiled=True),
        lax.all_gather(query_bias, "fsdp", axis=0, tiled=True),
        lax.all_gather(key_weight, "fsdp", axis=0, tiled=True),
        lax.all_gather(value_weight, "fsdp", axis=0, tiled=True),
        lax.all_gather(value_bias, "fsdp", axis=0, tiled=True),
        lax.all_gather(out_weight, "fsdp", axis=0, tiled=True),
        lax.all_gather(out_bias, "fsdp", axis=0, tiled=True),
        lax.all_gather(first_gain, "fsdp", axis=0, tiled=True),
        lax.all_gather(first_shift, "fsdp", axis=0, tiled=True),
    )
    first_grad, grad_first_gain, grad_first_shift = norm_back(
        hidden_grad, first_normed, first_rescale, attention_back[7]
    )
    out_grad = first_grad.astype(jnp.bfloat16)
    grad_out = weight_grad(mixed, out_grad)
    grad_out_bias = bias_grad(out_grad)
    mixed_grad = back_rows(out_grad, attention_back[5]).astype(jnp.bfloat16).reshape(shaped)
    query_grad, key_grad, value_grad = lax.map(
        attend_backward, (queries, key_rows, value_rows, segment_ids, mixed_grad, log_totals)
    )
    query_grad = query_grad.reshape(tokens.shape)
    key_grad = key_grad.reshape(tokens.shape)
    value_grad = value_grad.reshape(tokens.shape)
    grad_query = weight_grad(tokens, query_grad)
    grad_query_bias = bias_grad(query_grad)
    grad_key = weight_grad(tokens, key_grad)
    grad_value = weight_grad(tokens, value_grad)
    grad_value_bias = bias_grad(value_grad)
    input_grad = (
        first_grad
        + back_rows(query_grad, attention_back[0])
        + back_rows(key_grad, attention_back[2])
        + back_rows(value_grad, attention_back[3])
    )
    attention_grads = (
        lax.psum_scatter(
            grad_query.astype(jnp.bfloat16), "fsdp", scatter_dimension=0, tiled=True
        ).astype(jnp.float32),
        lax.psum_scatter(
            grad_query_bias.astype(jnp.bfloat16), "fsdp", scatter_dimension=0, tiled=True
        ).astype(jnp.float32),
        lax.psum_scatter(
            grad_key.astype(jnp.bfloat16), "fsdp", scatter_dimension=0, tiled=True
        ).astype(jnp.float32),
        lax.psum_scatter(
            grad_value.astype(jnp.bfloat16), "fsdp", scatter_dimension=0, tiled=True
        ).astype(jnp.float32),
        lax.psum_scatter(
            grad_value_bias.astype(jnp.bfloat16), "fsdp", scatter_dimension=0, tiled=True
        ).astype(jnp.float32),
        lax.psum_scatter(
            grad_out.astype(jnp.bfloat16), "fsdp", scatter_dimension=0, tiled=True
        ).astype(jnp.float32),
        lax.psum_scatter(
            grad_out_bias.astype(jnp.bfloat16), "fsdp", scatter_dimension=0, tiled=True
        ).astype(jnp.float32),
        lax.psum_scatter(
            grad_first_gain.astype(jnp.bfloat16), "fsdp", scatter_dimension=0, tiled=True
        ).astype(jnp.float32),
        lax.psum_scatter(
            grad_first_shift.astype(jnp.bfloat16), "fsdp", scatter_dimension=0, tiled=True
        ).astype(jnp.float32),
    )
    summed = (
        lax.psum(attention_grads[0].astype(jnp.bfloat16), "dp").astype(jnp.float32),
        lax.psum(attention_grads[1].astype(jnp.bfloat16), "dp").astype(jnp.float32),
        lax.psum(attention_grads[2].astype(jnp.bfloat16), "dp").astype(jnp.float32),
        lax.psum(attention_grads[3].astype(jnp.bfloat16), "dp").astype(jnp.float32),
        lax.psum(attention_grads[4].astype(jnp.bfloat16), "dp").astype(jnp.float32),
        lax.psum(attention_grads[5].astype(jnp.bfloat16), "dp").astype(jnp.float32),
        lax.psum(attention_grads[6].astype(jnp.bfloat16), "dp").astype(jnp.float32),
        lax.psum(attention_grads[7].astype(jnp.bfloat16), "dp").astype(jnp.float32),
        lax.psum(attention_grads[8].astype(jnp.bfloat16), "dp").astype(jnp.float32),
        lax.psum(feed_grads[0].astype(jnp.bfloat16), "dp").astype(jnp.float32),
        lax.psum(feed_grads[1].astype(jnp.bfloat16), "dp").astype(jnp.float32),
        lax.psum(feed_grads[2].astype(jnp.bfloat16), "dp").astype(jnp.float32),
        lax.psum(feed_grads[3].astype(jnp.bfloat16), "dp").astype(jnp.float32),
        lax.psum(feed_grads[4].astype(jnp.bfloat16), "dp").astype(jnp.float32),
        lax.psum(feed_grads[5].astype(jnp.bfloat16), "dp").astype(jnp.float32),
    )
    return (
        output.astype(jnp.bfloat16),
        input_grad,
        summed[0],
        summed[1],
        summed[2],
        summed[3],
        summed[4],
        summed[5],
        summed[6],
        summed[7],
        summed[8],
        summed[9],
        summed[10],
        summed[11],
        summed[12],
        summed[13],
        summed[14],
    )


def solution(mesh):
    in_specs = (
        P(("dp", "fsdp"), None),
        P(("dp", "fsdp"), None),
        P("fsdp", None),
        P("fsdp"),
        P("fsdp", None),
        P("fsdp", None),
        P("fsdp"),
        P("fsdp", None),
        P("fsdp"),
        P("fsdp"),
        P("fsdp"),
        P("fsdp", None),
        P("fsdp"),
        P("fsdp", None),
        P("fsdp"),
        P("fsdp"),
        P("fsdp"),
        P(("dp", "fsdp"), None),
    )
    out_specs = (
        P(("dp", "fsdp"), None),
        P(("dp", "fsdp"), None),
        P("fsdp", None),
        P("fsdp"),
        P("fsdp", None),
        P("fsdp", None),
        P("fsdp"),
        P("fsdp", None),
        P("fsdp"),
        P("fsdp"),
        P("fsdp"),
        P("fsdp", None),
        P("fsdp"),
        P("fsdp", None),
        P("fsdp"),
        P("fsdp"),
        P("fsdp"),
    )
    return jax.shard_map(
        on_device, mesh=mesh, in_specs=in_specs, out_specs=out_specs, check_vma=False
    )
```

profile of v0, /device:TPU:0, one launch (start us, length us, event | category | flops | bytes accessed | tf_op | source)
XLA Modules:
  0.0 987.1 jit_solution(2345672940246471056)
XLA Ops:
  19.1 39.4 %all-reduce.18 = (bf16[768]{0:T(1024)(128)(2,1)S(1)}, bf16[768]{0:T(1024)(128)(2,1)S(1)}, bf16[768]{0:T(1024)(128)(2,1)S(1)}, bf16[768]{0:T(1024)(128)(2,1)S(1)}...) all-reduce(bf16[768]{0:T(1024)(128)(2,1)S(1)} %dynamic-update-slice, ...), channel_id=1, replica_groups=mesh['dp'=4,'fsdp'=8] {'fsdp'}, use_global_device_ids=true, to_apply=%add.1 | all-reduce | flops 5376 | bytes 21504
  61.2 26.2 %all-gather = bf16[8,1,384]{2,1,0:T(2,128)(2,1)S(1)} all-gather(bf16[1,1,384]{2,1,0:T(2,128)(2,1)S(1)} %reshape.227), channel_id=1, replica_groups=mesh['dp'=4,'fsdp'=8] {'fsdp'}, dimensions={0}, use_global_device_ids=true | all-gather | bytes 6912 | tf_op jit(solution)/shard_map/all_gather | solution.py:146
  103.7 34.7 %all-gather.12.cloned.1.call-done = bf16[768,768]{1,0:T(8,128)(2,1)} async-done(((bf16[96,768]{1,0:T(8,128)(2,1)}), bf16[768,768]{1,0:T(8,128)(2,1)}) %all-gather.12.cloned.1.call-update) | async-done | bytes 1179664 | tf_op jit(solution)/shard_map/all_gather | solution.py:120
  149.9 21.0 %while.26 = (s32[]{:T(128)}, bf16[2,512,12,64]{1,3,2,0:T(8,128)(2,1)}, f32[2,12,512,1]{2,1,3,0:T(8,128)S(1)}, bf16[2,512,12,64]{1,3,2,0:T(8,128)(2,1)}, s32[2,51...) while((s32[]{:T(128)}, ...), condition=%wide.region_3.4_spmd, body=%wide.region_0.3_spmd.sunk | while | flops 843704320 | bytes 42172508 | solution.py:139
  186.2 74.1 %all-gather.16.cloned.1.call-done = bf16[768,3072]{1,0:T(8,128)(2,1)} async-done(((bf16[96,3072]{1,0:T(8,128)(2,1)}), bf16[768,3072]{1,0:T(8,128)(2,1)}) %all-gather.16.cloned.1.call-update) | async-done | bytes 4718608 | tf_op jit(solution)/shard_map/all_gather | solution.py:145
  260.4 50.1 %fusion.59 = (bf16[1024,3072]{1,0:T(8,128)(2,1)}, f32[1024,3072]{1,0:T(8,128)}) fusion(f32[3072]{0:T(1024)S(1)} %bitcast.193, bf16[768,3072]{1,0:T(8,128)(2,1)} %all-gather.16.cloned.1.call-done, f32[1024,768]{0,1:T(8,128)} %copy-done.7, f32[768]{0:T(1024)S(1)} %convert_element_type.228, f32[768]{0:T(1024)S(1)} %convert_element_type.227, ...), kind=kOutput, calls=%fused_computation.68 | convolution fusion | flops 5043388416 | bytes 26765312 | tf_op jit(solution)/shard_map/dot_general | solution.py:26
  310.5 29.6 %all-gather.18.cloned.1.call-done = bf16[3072,768]{1,0:T(8,128)(2,1)} async-done(((bf16[384,768]{1,0:T(8,128)(2,1)}), bf16[3072,768]{1,0:T(8,128)(2,1)}) %all-gather.18.cloned.1.call-update) | async-done | bytes 4718608 | tf_op jit(solution)/shard_map/all_gather | solution.py:147
  340.1 9.4 fusion.94
  356.0 14.7 %fusion.95 = (bf16[3072]{0:T(1024)(128)(2,1)}, bf16[1024,3072]{1,0:T(8,128)(2,1)}) fusion(f32[1024,3072]{1,0:T(8,128)} %get-tuple-element.302, f32[3072]{0:T(1024)S(1)} %bitcast.194, bf16[1024,768]{0,1:T(8,128)(2,1)S(1)} %get-tuple-element.290, bf16[3072,768]{1,0:T(8,128)(2,1)S(1)} %bitcast.198), kind=kOutput, calls=%fused_computation.144 | convolution fusion | flops 4869583872 | bytes 25184256 | tf_op jit(solution)/shard_map/to,io->ti/dot_general | solution.py:38
  370.7 9.7 multiply_reduce_fusion.1
  399.9 48.5 %while.27 = (s32[]{:T(128)}, bf16[2,512,12,64]{1,3,2,0:T(8,128)(2,1)}, bf16[2,512,12,64]{1,3,2,0:T(8,128)(2,1)}, bf16[2,512,12,64]{1,3,2,0:T(8,128)(2,1)}, bf16[...) while((s32[]{:T(128)}, ...), condition=%wide.region_14.15_spmd, body=%wide.region_12.14_spmd.sunk | while | flops 2062673920 | bytes 134941968 | solution.py:212
  402.2 6.9 multiply_reduce_fusion.7
  409.1 7.1 multiply_convert_fusion.4
  426.3 6.9 multiply_reduce_fusion.7
  433.2 7.1 multiply_convert_fusion.4
  479.2 9.8 convolution_convert_fusion.1
  490.4 9.7 convolution_convert_fusion
  505.7 34.7 %all-reduce.17 = (bf16[768]{0:T(1024)(128)(2,1)S(1)}, bf16[768]{0:T(1024)(128)(2,1)S(1)}, bf16[768]{0:T(1024)(128)(2,1)S(1)}, bf16[768]{0:T(1024)(128)(2,1)S(1)}...) all-reduce(bf16[768]{0:T(1024)(128)(2,1)S(1)} %dynamic-update-slice, ...), channel_id=1, replica_groups=mesh['dp'=4,'fsdp'=8] {'fsdp'}, use_global_device_ids=true, to_apply=%add.7 | all-reduce | flops 9984 | bytes 39936
  560.8 27.7 %reduce-scatter.21.cloned.1.call-done = bf16[96,768]{1,0:T(8,128)(2,1)} async-done(((bf16[768,768]{1,0:T(8,128)(2,1)}), bf16[96,768]{1,0:T(8,128)(2,1)}) %reduce-scatter.21.cloned.1.call-update) | async-done | bytes 147472
  590.2 65.5 %reduce-scatter.23.cloned.1.call-done = bf16[96,768]{1,0:T(8,128)(2,1)} async-done(((bf16[768,768]{1,0:T(8,128)(2,1)}), bf16[96,768]{1,0:T(8,128)(2,1)}) %reduce-scatter.23.cloned.1.call-update) | async-done | bytes 147472
  657.5 65.9 %reduce-scatter.13.cloned.1.call-done = bf16[96,768]{1,0:T(8,128)(2,1)} async-done(((bf16[768,768]{1,0:T(8,128)(2,1)}), bf16[96,768]{1,0:T(8,128)(2,1)}) %reduce-scatter.13.cloned.1.call-update) | async-done | bytes 147472 | tf_op jit(solution)/shard_map/reduce_scatter | solution.py:245
  723.4 98.4 %reduce-scatter.15.cloned.1.call-done = bf16[96,3072]{1,0:T(8,128)(2,1)} async-done(((bf16[768,3072]{1,0:T(8,128)(2,1)}), bf16[96,3072]{1,0:T(8,128)(2,1)}) %reduce-scatter.15.cloned.1.call-update) | async-done | bytes 589840 | tf_op jit(solution)/shard_map/reduce_scatter | solution.py:175
  821.8 98.9 %reduce-scatter.17.cloned.1.call-done = bf16[384,768]{1,0:T(8,128)(2,1)} async-done(((bf16[3072,768]{1,0:T(8,128)(2,1)}), bf16[384,768]{1,0:T(8,128)(2,1)}) %reduce-scatter.17.cloned.1.call-update) | async-done | bytes 589840 | tf_op jit(solution)/shard_map/reduce_scatter | solution.py:181
  935.8 36.6 %all-reduce.23.cloned.1.call-done = (bf16[96,768]{0,1:T(8,128)(2,1)}, bf16[96,768]{0,1:T(8,128)(2,1)}, bf16[96,768]{0,1:T(8,128)(2,1)}, bf16[96,768]{1,0:T(8,128...) async-done(((bf16[96,768]{0,1:T(8,128)(2,1)}, bf16[96,768]{0,1:T(8,128)(2,1)}, bf16[96,768]{0,1:T(8,128)(2,1)}, bf16[96,768]{1,0:T(8,128)(2,1)}, ...) | async-done | bytes 1769488 | tf_op jit(solution)/shard_map/psum | solution.py:259
  (307 shorter events, 206.1 us)
Async XLA Ops:
  7.2 54.0 %copy-start.53 = (bf16[384]{0:T(512)(128)(2,1)S(1)}, bf16[384]{0:T(512)(128)(2,1)}, u32[]{:S(2)}) copy-start(bf16[384]{0:T(512)(128)(2,1)} %param.34) | copy-start | bytes 2308
  7.2 81.5 %copy-start.11 = (bf16[1024,768]{1,0:T(8,128)(2,1)S(1)}, bf16[1024,768]{1,0:T(8,128)(2,1)}, u32[]{:S(2)}) copy-start(bf16[1024,768]{1,0:T(8,128)(2,1)} %param.39) | copy-start | bytes 4718596
  7.2 83.1 %all-gather.8.cloned.1.call-start = ((), (), s32[]{:S(2)}) async-start(), calls=%async_computation.6 | async-start | bytes 1327104 | tf_op jit(solution)/shard_map/all_gather | solution.py:121
  7.9 90.6 %all-gather.10.cloned.1.call-start = ((), (), s32[]{:S(2)}) async-start(), calls=%async_computation.7 | async-start | bytes 1327104 | tf_op jit(solution)/shard_map/all_gather | solution.py:118
  8.7 129.7 %all-gather.12.cloned.1.call-start = ((), (), s32[]{:S(2)}) async-start(), calls=%async_computation.8 | async-start | bytes 1327104 | tf_op jit(solution)/shard_map/all_gather | solution.py:120
  9.4 170.9 %all-gather.14.cloned.1.call-start = ((), (), s32[]{:S(2)}) async-start(), calls=%async_computation.9 | async-start | bytes 1327104 | tf_op jit(solution)/shard_map/all_gather | solution.py:123
  10.0 250.4 %all-gather.16.cloned.1.call-start = ((), (), s32[]{:S(2)}) async-start(), calls=%async_computation.10 | async-start | bytes 5308416 | tf_op jit(solution)/shard_map/all_gather | solution.py:145
  10.6 329.5 %all-gather.18.cloned.1.call-start = ((), (), s32[]{:S(2)}) async-start(), calls=%async_computation.11 | async-start | bytes 5308416 | tf_op jit(solution)/shard_map/all_gather | solution.py:147
  11.2 547.9 %reduce-scatter.19.cloned.1.call-start = ((), (), s32[]{:S(2)}) async-start(), calls=%async_computation.15 | async-start | bytes 1327104
  58.5 31.8 %copy-start.17 = (bf16[1024,768]{1,0:T(8,128)(2,1)S(1)}, bf16[1024,768]{1,0:T(8,128)(2,1)}, u32[]{:S(2)}) copy-start(bf16[1024,768]{1,0:T(8,128)(2,1)} %param.22) | copy-start | bytes 4718596
  61.2 319.2 %copy-start.40 = (f32[768]{0:T(1024)}, f32[768]{0:T(1024)S(1)}, u32[]{:S(2)}) copy-start(f32[768]{0:T(1024)S(1)} %convert_element_type.227) | copy-start | bytes 9220
  61.2 278.9 %copy-start.48 = (f32[768]{0:T(1024)}, f32[768]{0:T(1024)S(1)}, u32[]{:S(2)}) copy-start(f32[768]{0:T(1024)S(1)} %convert_element_type.228) | copy-start | bytes 9220
  184.2 196.2 %copy-start.38 = (f32[1024]{0:T(1024)}, f32[1024]{0:T(1024)S(1)}, u32[]{:S(2)}) copy-start(f32[1024]{0:T(1024)S(1)} %broadcast_multiply_fusion.5) | copy-start | bytes 12292
  186.2 194.2 %copy-start.42 = (f32[1024]{0:T(1024)}, f32[1024]{0:T(1024)S(1)}, u32[]{:S(2)}) copy-start(f32[1024]{0:T(1024)S(1)} %add_rsqrt_fusion.1) | copy-start | bytes 12292
  260.4 79.8 %copy-start.50 = (f32[768]{0:T(1024)S(1)}, f32[768]{0:T(1024)}, u32[]{:S(2)}) copy-start(f32[768]{0:T(1024)} %convert_element_type.232) | copy-start | bytes 9220
  349.6 21.1 %copy-start = (f32[1024,768]{0,1:T(8,128)}, f32[1024,768]{0,1:T(8,128)S(1)}, u32[]{:S(2)}) copy-start(f32[1024,768]{0,1:T(8,128)S(1)} %get-tuple-element.304) | copy-start | bytes 9437188
  458.0 130.5 %reduce-scatter.21.cloned.1.call-start = ((), (), s32[]{:S(2)}) async-start(), calls=%async_computation.16 | async-start | bytes 1327104
  466.4 189.4 %reduce-scatter.23.cloned.1.call-start = ((), (), s32[]{:S(2)}) async-start(), calls=%async_computation.17 | async-start | bytes 1327104
  474.6 248.8 %reduce-scatter.13.cloned.1.call-start = ((), (), s32[]{:S(2)}) async-start(), calls=%async_computation.12 | async-start | bytes 1327104 | tf_op jit(solution)/shard_map/reduce_scatter | solution.py:245
  479.1 342.7 %reduce-scatter.15.cloned.1.call-start = ((), (), s32[]{:S(2)}) async-start(), calls=%async_computation.13 | async-start | bytes 5308416 | tf_op jit(solution)/shard_map/reduce_scatter | solution.py:175
  489.0 431.7 %reduce-scatter.17.cloned.1.call-start = ((), (), s32[]{:S(2)}) async-start(), calls=%async_computation.14 | async-start | bytes 5308416 | tf_op jit(solution)/shard_map/reduce_scatter | solution.py:181
  500.2 472.2 %all-reduce.23.cloned.1.call-start = ((), (), s32[]{:S(2)}) async-start(), calls=%async_computation.18 | async-start | bytes 3833856 | tf_op jit(solution)/shard_map/psum | solution.py:259
  501.8 49.6 %copy-start.22 = (bf16[96,8,2,512]{3,1,2,0:T(8,128)(2,1)S(1)}, bf16[96,8,2,512]{3,1,2,0:T(8,128)(2,1)}, u32[]{:S(2)}) copy-start(bf16[96,8,2,512]{3,1,2,0:T(8,128)(2,1)} %copy-done.21) | copy-start | bytes 4718596
  556.0 364.7 %copy-start.10 = (f32[1024,768]{0,1:T(8,128)S(1)}, f32[1024,768]{0,1:T(8,128)}, u32[]{:S(2)}) copy-start(f32[1024,768]{0,1:T(8,128)} %copy-done.9) | copy-start | bytes 9437188
  (55 other events, 278.8 us)
Sparse Core Ops, SparseCore 0:
  10.2 44.1 all-gather.7
  56.5 39.7 all-gather.9
  98.6 39.7 all-gather.11
  140.4 39.7 all-gather.13
  182.3 78.0 all-gather.15
  262.4 77.6 all-gather.17
  458.1 63.1 reduce-scatter.18
  524.7 63.7 reduce-scatter.20
  591.9 63.8 reduce-scatter.22
  659.6 63.8 reduce-scatter.12
  727.1 94.6 reduce-scatter.14
  825.3 95.3 reduce-scatter.16
  924.1 48.3 all-reduce.22
where the time goes:
time: 995 us; the launch traced here: 987 us
  waiting for transfers between devices  540 us (54%)
  matrix products  195 us (20%)
  blocking collectives  106 us (11%)
  local copies, waits for them, and re-layouts  85.5 us (9%)
  other arithmetic  41.6 us (4%)
  between operations  17.1 us (2%)
    reduce_scatter x1, waiting for transfers between devices, on_device(): lax.psum_scatter(grad_reduce.astype(jnp.bfloat16), 'fsdp', scatter_dimens...  98.9 us
    reduce_scatter x1, waiting for transfers between devices, on_device(): lax.psum_scatter(grad_expand.astype(jnp.bfloat16), 'fsdp', scatter_dimens...  98.4 us
    unnamed x16, waiting for transfers between devices  97 us
    all_gather x1, waiting for transfers between devices, on_device(): lax.all_gather(expand_weight, 'fsdp', axis=0, tiled=True)  74.1 us
    unnamed x2, blocking collectives  74 us
    dot_general x5, matrix products, linear(): jnp.dot(rows, weight, preferred_element_type=jnp.float32)  69.9 us
    reduce_scatter x1, waiting for transfers between devices, on_device(): lax.psum_scatter(grad_out.astype(jnp.bfloat16), 'fsdp', scatter_dimension...  65.9 us
    unnamed x156, local copies, waits for them, and re-layouts  48.6 us
  transfers between devices with their start and end apart: 13, of which 10 were waited for; matrix products, arithmetic and copies ran while one was open for 19% of the time, Pallas kernels for 0%

commit v1 on v0

--- a/solution.py
+++ b/solution.py
@@ -5,6 +5,28 @@
 
 HEADS = 12
 HEAD = 64
+
+
+def in_order(parts, dim):
+    parts = jnp.moveaxis(parts, 0, dim)
+    dims = parts.shape
+    return parts.reshape(*dims[:dim], dims[dim] * dims[dim + 1], *dims[dim + 2 :])
+
+
+def collect(array, axis, dim):
+    size = lax.axis_size(axis)
+    pairs = [(i, (i + 1) % size) for i in range(size)]
+    back = [(b, a) for a, b in pairs]
+    lower, upper = ([], [])
+    for step in range(size - 1):
+        if step % 2 == 0:
+            lower.append(lax.ppermute(lower[-1] if lower else array, axis, pairs))
+        else:
+            upper.append(lax.ppermute(upper[-1] if upper else array, axis, back))
+    tiles = jnp.stack([*lower[::-1], array, *upper])
+    shift = lax.axis_index(axis) - len(lower)
+    tiles = tiles[(jnp.arange(size) - shift) % size]
+    return in_order(tiles, dim)
 
 
 def layer_norm(rows, gain, shift):
@@ -117,7 +139,7 @@
     attention_set = (
         lax.all_gather(query_weight, "fsdp", axis=0, tiled=True),
         lax.all_gather(query_bias, "fsdp", axis=0, tiled=True),
-        lax.all_gather(key_weight, "fsdp", axis=0, tiled=True),
+        collect(key_weight, "fsdp", 0),
         lax.all_gather(value_weight, "fsdp", axis=0, tiled=True),
         lax.all_gather(value_bias, "fsdp", axis=0, tiled=True),
         lax.all_gather(out_weight, "fsdp", axis=0, tiled=True),

time: 995 us -> 956 us (0.961)
  waiting for transfers between devices: 540 us -> 485 us
  starting transfers between devices: 0.98 us -> 13.6 us
    all_gather x1, waiting for transfers between devices: 34.7 us -> 0.01 us  [on_device(): lax.all_gather(key_weight, 'fsdp', axis=0, tiled=True)]
    all_gather x1, waiting for transfers between devices: 74.1 us -> 41.2 us  [on_device(): lax.all_gather(expand_weight, 'fsdp', axis=0, tiled=True)]
    ppermute x0 -> x7, waiting for transfers between devices: none -> 18.6 us  [the longest x4 16.3 us: collect(): lower.append(lax.ppermute(lower[-1] if lower else array, axis, pairs))]
    ppermute x0 -> x7, starting transfers between devices: none -> 12.6 us  [the longest x3 9.55 us: collect(): upper.append(lax.ppermute(upper[-1] if upper else array, axis, back))]
    unnamed x156 -> x161, local copies, waits for them, and re-layouts: 48.6 us -> 50.6 us
  transfers between devices with their start and end apart: 13 -> 20, of which waited for: 10 -> 12; matrix products, arithmetic and copies ran while one was open for 19% -> 33% of each run, Pallas kernels for 0% -> 0%
where the time goes in v1:
time: 956 us; the launch traced here: 950 us
  waiting for transfers between devices  485 us (51%)
  matrix products  196 us (21%)
  blocking collectives  104 us (11%)
  local copies, waits for them, and re-layouts  91.3 us (10%)
  other arithmetic  41.6 us (4%)
  between operations  17.2 us (2%)
  starting transfers between devices  13.6 us (1%)
    reduce_scatter x1, waiting for transfers between devices, on_device(): lax.psum_scatter(grad_expand.astype(jnp.bfloat16), 'fsdp', scatter_dimens...  98.9 us
    reduce_scatter x1, waiting for transfers between devices, on_device(): lax.psum_scatter(grad_reduce.astype(jnp.bfloat16), 'fsdp', scatter_dimens...  98.4 us
    unnamed x16, waiting for transfers between devices  95.7 us
    unnamed x2, blocking collectives  72.3 us
    dot_general x5, matrix products, linear(): jnp.dot(rows, weight, preferred_element_type=jnp.float32)  71.5 us
    reduce_scatter x1, waiting for transfers between devices, on_device(): lax.psum_scatter(grad_out.astype(jnp.bfloat16), 'fsdp', scatter_dimension...  65.9 us
    unnamed x161, local copies, waits for them, and re-layouts  50.6 us
    dot_general x6, matrix products, back_rows(): jnp.einsum('to,io->ti', gradient, weight, preferred_element_type=jnp.floa...  43.2 us
  transfers between devices with their start and end apart: 20, of which 12 were waited for; matrix products, arithmetic and copies ran while one was open for 33% of the time, Pallas kernels for 0%

profile of v1, /device:TPU:0, one launch (start us, length us, event | category | flops | bytes accessed | tf_op | source)
XLA Modules:
  0.0 949.8 jit_solution(11030017601277436776)
XLA Ops:
  13.7 7.1 collective-permute-done
  47.4 37.6 %all-reduce.18 = (bf16[768]{0:T(1024)(128)(2,1)S(1)}, bf16[768]{0:T(1024)(128)(2,1)S(1)}, bf16[768]{0:T(1024)(128)(2,1)S(1)}, bf16[768]{0:T(1024)(128)(2,1)S(1)}...) all-reduce(bf16[768]{0:T(1024)(128)(2,1)S(1)} %dynamic-update-slice, ...), channel_id=1, replica_groups=mesh['dp'=4,'fsdp'=8] {'fsdp'}, use_global_device_ids=true, to_apply=%add.1 | all-reduce | flops 5376 | bytes 21504
  87.7 26.1 %all-gather = bf16[8,1,384]{2,1,0:T(2,128)(2,1)S(1)} all-gather(bf16[1,1,384]{2,1,0:T(2,128)(2,1)S(1)} %reshape.288), channel_id=1, replica_groups=mesh['dp'=4,'fsdp'=8] {'fsdp'}, dimensions={0}, use_global_device_ids=true | all-gather | bytes 6912 | tf_op jit(solution)/shard_map/all_gather | solution.py:168
  150.7 20.7 %while.26 = (s32[]{:T(128)}, bf16[2,512,12,64]{1,3,2,0:T(8,128)(2,1)}, f32[2,12,512,1]{2,1,3,0:T(8,128)S(1)}, bf16[2,512,12,64]{1,3,2,0:T(8,128)(2,1)}, s32[2,51...) while((s32[]{:T(128)}, ...), condition=%wide.region_3.4_spmd, body=%wide.region_0.3_spmd.sunk | while | flops 843704320 | bytes 42172508 | solution.py:161
  182.0 41.2 %all-gather.14.cloned.1.call-done = bf16[768,3072]{1,0:T(8,128)(2,1)} async-done(((bf16[96,3072]{1,0:T(8,128)(2,1)}), bf16[768,3072]{1,0:T(8,128)(2,1)}) %all-gather.14.cloned.1.call-update) | async-done | bytes 4718608 | tf_op jit(solution)/shard_map/all_gather | solution.py:167
  223.2 50.0 %fusion.59 = (bf16[1024,3072]{1,0:T(8,128)(2,1)}, f32[1024,3072]{1,0:T(8,128)}) fusion(f32[3072]{0:T(1024)S(1)} %bitcast.215, bf16[768,3072]{1,0:T(8,128)(2,1)} %all-gather.14.cloned.1.call-done, f32[1024,768]{0,1:T(8,128)} %copy-done.7, f32[768]{0:T(1024)S(1)} %convert_element_type.232, f32[768]{0:T(1024)S(1)} %convert_element_type.231, ...), kind=kOutput, calls=%fused_computation.69 | convolution fusion | flops 5043388416 | bytes 26765312 | tf_op jit(solution)/shard_map/dot_general | solution.py:48
  273.2 29.7 %all-gather.16.cloned.1.call-done = bf16[3072,768]{1,0:T(8,128)(2,1)} async-done(((bf16[384,768]{1,0:T(8,128)(2,1)}), bf16[3072,768]{1,0:T(8,128)(2,1)}) %all-gather.16.cloned.1.call-update) | async-done | bytes 4718608 | tf_op jit(solution)/shard_map/all_gather | solution.py:169
  302.9 9.4 fusion.97
  318.8 14.7 %fusion.98 = (bf16[3072]{0:T(1024)(128)(2,1)}, bf16[1024,3072]{1,0:T(8,128)(2,1)}) fusion(f32[1024,3072]{1,0:T(8,128)} %get-tuple-element.302, f32[3072]{0:T(1024)S(1)} %bitcast.216, bf16[1024,768]{0,1:T(8,128)(2,1)S(1)} %get-tuple-element.290, bf16[3072,768]{1,0:T(8,128)(2,1)S(1)} %bitcast.220), kind=kOutput, calls=%fused_computation.161 | convolution fusion | flops 4869583872 | bytes 25184256 | tf_op jit(solution)/shard_map/to,io->ti/dot_general | solution.py:60
  333.5 9.7 %multiply_reduce_fusion.1 = (bf16[768]{0:T(1024)(128)(2,1)}, f32[1024]{0:T(1024)S(1)}, f32[1024]{0:T(1024)S(1)}, bf16[768]{0:T(1024)(128)(2,1)}, f32[1024,768]{0,1:T(8,128)S(1)}) fusion(f32[1024,768]{0,1:T(8,128)S(1)} %copy-done.8, f32[1024]{0:T(1024)S(1)} %add_rsqrt_fusion.1, f32[1024]{0:T(1024)S(1)} %broadcast_multiply_fusion.5, ...), kind=kOutput, calls=%fused_computation.102 | convolution fusion | flops 4845989888 | bytes 22062080 | tf_op jit(solution)/shard_map/to,io->ti/dot_general | solution.py:60
  362.7 48.4 %while.27 = (s32[]{:T(128)}, bf16[2,512,12,64]{1,3,2,0:T(8,128)(2,1)}, bf16[2,512,12,64]{1,3,2,0:T(8,128)(2,1)}, bf16[2,512,12,64]{1,3,2,0:T(8,128)(2,1)}, bf16[...) while((s32[]{:T(128)}, ...), condition=%wide.region_14.15_spmd, body=%wide.region_12.14_spmd.sunk | while | flops 2062673920 | bytes 134941968 | solution.py:234
  365.0 6.9 multiply_reduce_fusion.7
  371.9 7.1 multiply_convert_fusion.4
  389.1 6.9 multiply_reduce_fusion.7
  396.0 7.1 multiply_convert_fusion.4
  441.9 9.1 convolution_convert_fusion
  451.7 9.8 %convolution_convert_fusion.1 = bf16[768,3072]{1,0:T(8,128)(2,1)} fusion(bf16[1024,3072]{1,0:T(8,128)(2,1)} %get-tuple-element.307, f32[1024,768]{0,1:T(8,128)} %copy-done.7, f32[768]{0:T(1024)S(1)} %copy-done.49, f32[768]{0:T(1024)S(1)} %copy-done.41, f32[1024]{0:T(1024)S(1)} %copy-done.43, f32[1024]{0:T(1024)S(1)} %copy-done.39), kind=kOutput, calls=%fused_computation.92 | convolution fusion | flops 4838129664 | bytes 14170112 | tf_op jit(solution)/shard_map/ti,to->io/dot_general | solution.py:52
  467.0 34.7 %all-reduce.17 = (bf16[768]{0:T(1024)(128)(2,1)S(1)}, bf16[768]{0:T(1024)(128)(2,1)S(1)}, bf16[768]{0:T(1024)(128)(2,1)S(1)}, bf16[768]{0:T(1024)(128)(2,1)S(1)}...) all-reduce(bf16[768]{0:T(1024)(128)(2,1)S(1)} %dynamic-update-slice, ...), channel_id=1, replica_groups=mesh['dp'=4,'fsdp'=8] {'fsdp'}, use_global_device_ids=true, to_apply=%add.7 | all-reduce | flops 9984 | bytes 39936
  524.4 27.0 %reduce-scatter.21.cloned.1.call-done = bf16[96,768]{1,0:T(8,128)(2,1)} async-done(((bf16[768,768]{1,0:T(8,128)(2,1)}), bf16[96,768]{1,0:T(8,128)(2,1)}) %reduce-scatter.21.cloned.1.call-update) | async-done | bytes 147472
  553.1 65.5 %reduce-scatter.23.cloned.1.call-done = bf16[96,768]{1,0:T(8,128)(2,1)} async-done(((bf16[768,768]{1,0:T(8,128)(2,1)}), bf16[96,768]{1,0:T(8,128)(2,1)}) %reduce-scatter.23.cloned.1.call-update) | async-done | bytes 147472
  620.3 65.9 %reduce-scatter.13.cloned.1.call-done = bf16[96,768]{1,0:T(8,128)(2,1)} async-done(((bf16[768,768]{1,0:T(8,128)(2,1)}), bf16[96,768]{1,0:T(8,128)(2,1)}) %reduce-scatter.13.cloned.1.call-update) | async-done | bytes 147472 | tf_op jit(solution)/shard_map/reduce_scatter | solution.py:267
  686.2 98.4 %reduce-scatter.17.cloned.1.call-done = bf16[384,768]{1,0:T(8,128)(2,1)} async-done(((bf16[3072,768]{1,0:T(8,128)(2,1)}), bf16[384,768]{1,0:T(8,128)(2,1)}) %reduce-scatter.17.cloned.1.call-update) | async-done | bytes 589840 | tf_op jit(solution)/shard_map/reduce_scatter | solution.py:203
  784.5 98.9 %reduce-scatter.15.cloned.1.call-done = bf16[96,3072]{1,0:T(8,128)(2,1)} async-done(((bf16[768,3072]{1,0:T(8,128)(2,1)}), bf16[96,3072]{1,0:T(8,128)(2,1)}) %reduce-scatter.15.cloned.1.call-update) | async-done | bytes 589840 | tf_op jit(solution)/shard_map/reduce_scatter | solution.py:197
  898.5 36.6 %all-reduce.23.cloned.1.call-done = (bf16[96,768]{0,1:T(8,128)(2,1)}, bf16[96,768]{0,1:T(8,128)(2,1)}, bf16[96,768]{0,1:T(8,128)(2,1)}, bf16[96,768]{1,0:T(8,128...) async-done(((bf16[96,768]{0,1:T(8,128)(2,1)}, bf16[96,768]{0,1:T(8,128)(2,1)}, bf16[96,768]{0,1:T(8,128)(2,1)}, bf16[96,768]{1,0:T(8,128)(2,1)}, ...) | async-done | bytes 1769488 | tf_op jit(solution)/shard_map/psum | solution.py:281
  (329 shorter events, 233.1 us)
Async XLA Ops:
  7.2 121.0 %all-gather.8.cloned.1.call-start = ((), (), s32[]{:S(2)}) async-start(), calls=%async_computation.6 | async-start | bytes 1327104 | tf_op jit(solution)/shard_map/all_gather | solution.py:143
  7.9 131.8 %all-gather.10.cloned.1.call-start = ((), (), s32[]{:S(2)}) async-start(), calls=%async_computation.7 | async-start | bytes 1327104 | tf_op jit(solution)/shard_map/all_gather | solution.py:140
  8.7 167.3 %all-gather.12.cloned.1.call-start = ((), (), s32[]{:S(2)}) async-start(), calls=%async_computation.8 | async-start | bytes 1327104 | tf_op jit(solution)/shard_map/all_gather | solution.py:145
  9.4 213.7 %all-gather.14.cloned.1.call-start = ((), (), s32[]{:S(2)}) async-start(), calls=%async_computation.9 | async-start | bytes 5308416 | tf_op jit(solution)/shard_map/all_gather | solution.py:167
  10.0 292.9 %all-gather.16.cloned.1.call-start = ((), (), s32[]{:S(2)}) async-start(), calls=%async_computation.10 | async-start | bytes 5308416 | tf_op jit(solution)/shard_map/all_gather | solution.py:169
  10.6 507.1 %all-gather.18.cloned.1.call-start = ((), (), s32[]{:S(2)}) async-start(), calls=%async_computation.11 | async-start | bytes 1327104 | tf_op jit(solution)/shard_map/all_gather | solution.py:219
  10.6 10.1 %collective-permute-start = (bf16[96,768]{1,0:T(8,128)(2,1)}, bf16[96,768]{1,0:T(8,128)(2,1)S(1)}, u32[]{:S(2)}, u32[]{:S(2)}) collective-permute-start(bf16[96,768]{1,0:T(8,128)(2,1)} %param.26), channel_id=1, source_target_pairs={{0,1},{1,2},{2,3},{3,4},{4,5},{5,6},{6,7},{7,0},{8,9},{9,10},{10,1... | collective-permute-start | bytes 442376 | tf_op jit(solution)/shard_map/ppermute | solution.py:23
  20.8 10.9 %collective-permute-start.1 = (bf16[96,768]{1,0:T(8,128)(2,1)S(1)}, bf16[96,768]{1,0:T(8,128)(2,1)S(1)}, u32[]{:S(2)}, u32[]{:S(2)}) collective-permute-start(bf16[96,768]{1,0:T(8,128)(2,1)S(1)} %collective-permute-done), channel_id=1, source_target_pairs={{0,1},{1,2},{2,3},{3,4},{4,5},{5,6},{6,7},{7,0},{8,9},{9,10},{10,1... | collective-permute-start | bytes 442376 | tf_op jit(solution)/shard_map/ppermute | solution.py:23
  20.8 11.0 %collective-permute-start.4 = (bf16[96,768]{1,0:T(8,128)(2,1)}, bf16[96,768]{1,0:T(8,128)(2,1)S(1)}, u32[]{:S(2)}, u32[]{:S(2)}) collective-permute-start(bf16[96,768]{1,0:T(8,128)(2,1)} %param.26), channel_id=1, source_target_pairs={{1,0},{2,1},{3,2},{4,3},{5,4},{6,5},{7,6},{0,7},{9,8},{10,9},{11,1... | collective-permute-start | bytes 442376 | tf_op jit(solution)/shard_map/ppermute | solution.py:25
  31.7 7.8 collective-permute-start.2
  31.7 490.9 %reduce-scatter.19.cloned.1.call-start = ((), (), s32[]{:S(2)}) async-start(), calls=%async_computation.15 | async-start | bytes 1327104
  31.8 84.9 %collective-permute-start.5 = (bf16[96,768]{1,0:T(8,128)(2,1)S(1)}, bf16[96,768]{1,0:T(8,128)(2,1)}, u32[]{:S(2)}, u32[]{:S(2)}) collective-permute-start(bf16[96,768]{1,0:T(8,128)(2,1)S(1)} %collective-permute-done.4), channel_id=1, source_target_pairs={{1,0},{2,1},{3,2},{4,3},{5,4},{6,5},{7,6},{0,7},{9,8},{10,9},{11,1... | collective-permute-start | bytes 442376 | tf_op jit(solution)/shard_map/ppermute | solution.py:25
  39.5 77.2 %collective-permute-start.3 = (bf16[96,768]{1,0:T(8,128)(2,1)S(1)}, bf16[96,768]{1,0:T(8,128)(2,1)}, u32[]{:S(2)}, u32[]{:S(2)}) collective-permute-start(bf16[96,768]{1,0:T(8,128)(2,1)S(1)} %collective-permute-done.2), channel_id=1, source_target_pairs={{0,1},{1,2},{2,3},{3,4},{4,5},{5,6},{6,7},{7,0},{8,9},{9,10},{10,1... | collective-permute-start | bytes 442376 | tf_op jit(solution)/shard_map/ppermute | solution.py:23
  87.7 255.5 %copy-start.40 = (f32[768]{0:T(1024)}, f32[768]{0:T(1024)S(1)}, u32[]{:S(2)}) copy-start(f32[768]{0:T(1024)S(1)} %convert_element_type.231) | copy-start | bytes 9220
  87.7 215.2 %copy-start.48 = (f32[768]{0:T(1024)}, f32[768]{0:T(1024)S(1)}, u32[]{:S(2)}) copy-start(f32[768]{0:T(1024)S(1)} %convert_element_type.232) | copy-start | bytes 9220
  116.7 5.4 collective-permute-start.6
  179.9 163.3 %copy-start.38 = (f32[1024]{0:T(1024)}, f32[1024]{0:T(1024)S(1)}, u32[]{:S(2)}) copy-start(f32[1024]{0:T(1024)S(1)} %broadcast_multiply_fusion.5) | copy-start | bytes 12292
  420.8 130.6 %reduce-scatter.21.cloned.1.call-start = ((), (), s32[]{:S(2)}) async-start(), calls=%async_computation.16 | async-start | bytes 1327104
  429.2 189.4 %reduce-scatter.23.cloned.1.call-start = ((), (), s32[]{:S(2)}) async-start(), calls=%async_computation.17 | async-start | bytes 1327104
  437.4 248.8 %reduce-scatter.13.cloned.1.call-start = ((), (), s32[]{:S(2)}) async-start(), calls=%async_computation.12 | async-start | bytes 1327104 | tf_op jit(solution)/shard_map/reduce_scatter | solution.py:267
  441.8 342.7 %reduce-scatter.17.cloned.1.call-start = ((), (), s32[]{:S(2)}) async-start(), calls=%async_computation.14 | async-start | bytes 5308416 | tf_op jit(solution)/shard_map/reduce_scatter | solution.py:203
  451.0 432.4 %reduce-scatter.15.cloned.1.call-start = ((), (), s32[]{:S(2)}) async-start(), calls=%async_computation.13 | async-start | bytes 5308416 | tf_op jit(solution)/shard_map/reduce_scatter | solution.py:197
  461.6 473.6 %all-reduce.23.cloned.1.call-start = ((), (), s32[]{:S(2)}) async-start(), calls=%async_computation.18 | async-start | bytes 3833856 | tf_op jit(solution)/shard_map/psum | solution.py:281
  517.7 365.8 %copy-start.10 = (f32[1024,768]{0,1:T(8,128)S(1)}, f32[1024,768]{0,1:T(8,128)}, u32[]{:S(2)}) copy-start(f32[1024,768]{0,1:T(8,128)} %copy-done.9) | copy-start | bytes 9437188
  (61 other events, 872.4 us)
Sparse Core Ops, SparseCore 0:
  10.2 48.5 all-gather.7
  60.9 39.5 all-gather.9
  102.7 40.2 all-gather.11
  145.1 78.0 all-gather.13
  225.2 77.6 all-gather.15
  305.0 39.4 all-gather.17
  420.9 63.2 reduce-scatter.18
  487.6 63.7 reduce-scatter.20
  554.8 63.7 reduce-scatter.22
  622.4 63.7 reduce-scatter.12
  689.8 94.6 reduce-scatter.16
  788.0 95.3 reduce-scatter.14
  886.8 48.3 all-reduce.22
